TPU v7x, 32 devices: a whole 2x2x4 slice. The times are simulated.
32 devices in a mesh: blk: 4 (over z), head: 2 (over core), clip: 4 (over y, x).
Axes of the slice: x: 2, y: 2, z: 4, core: 2. Of those that a mesh axis runs over, the one named last changes fastest.
Arguments:
- tokens: bfloat16 [4608, 1536], P(('clip', 'blk', 'head')), parts along dimension 0, may hold values from -6 to 6
- modulation: float32 [12, 1536], P('clip'), parts along dimension 0, may hold values from -3 to 3
- w_qkv: bfloat16 [1536, 3, 1536], P(None, None, 'head'), may hold values from -0.25 to 0.25
- w_out: bfloat16 [1536, 1536], P('head'), may hold values from -0.15625 to 0.15625
- w_cross: bfloat16 [1536, 1536], P(None, 'head'), may hold values from -0.15625 to 0.15625
- q_gain: float32 [128], replicated, may hold values from 0.5 to 6
- k_gain: float32 [128], replicated, may hold values from 0.5 to 6
- cross_gain: float32 [128], replicated, may hold values from 0.5 to 6
- scene_keys: bfloat16 [1024, 1536], P(('clip', 'blk'), 'head'), parts along dimension 0, may hold values from -40 to 40
- scene_values: bfloat16 [1024, 1536], P(('clip', 'blk'), 'head'), parts along dimension 0, may hold values from -6 to 6
Outputs:
- hidden: bfloat16 [4608, 1536], P(('clip', 'blk', 'head')), parts along dimension 0
- cross_context: bfloat16 [4608, 1536], P(('clip', 'blk'), 'head'), parts along dimension 0
There are 4 independent parts, one for each index of `clip`. A program takes and returns all parts, laid end to end along the dimension named above; an argument that names none is the same for every part. Nothing has to cross between parts.
All inputs are finite; a program needn't handle non-finite values.
Results may differ from a plain program's by a relative error of at most 0.015.
The roundings to bfloat16 on the way count: a program that leaves them out, or rounds other values in their place, can miss the bound.
Values may be sent and summed in bfloat16 or wider, within the bound.
No kernel may reach another device: no remote copies, remote signals or barrier semaphores. Data moves between devices by JAX's collectives and lax.ppermute only.
A program may use at most 128 MiB of HBM per device.

v0:
```python
import jax
import jax.numpy as jnp
from jax import lax
from jax.sharding import PartitionSpec as P

HD = 128


def head_norm(values, gain):
    rms = jnp.mean(values * values, axis=-1, keepdims=True)
    return values * lax.rsqrt(rms + 1e-06) * gain


def attend_block(carry, queries, keys_blk, values_blk):
    best, total, accum = carry
    count = keys_blk.shape[0]
    heads_here = queries.shape[1]
    width = queries.shape[2]
    keys_three = keys_blk.reshape(count, heads_here, width)
    values_three = values_blk.reshape(count, heads_here, width).astype(jnp.float32)
    scores = jnp.einsum("rhd,nhd->hrn", queries, keys_three, preferred_element_type=jnp.float32) * (
        1.0 / width**0.5
    )
    newbest = jnp.maximum(best, jnp.max(scores, axis=-1))
    factor = jnp.exp(best - newbest)
    weights = jnp.exp(scores - newbest[..., None])
    total = total * factor + jnp.sum(weights, axis=-1)
    accum = accum * jnp.transpose(factor)[..., None] + jnp.einsum(
        "hrn,nhd->rhd", weights, values_three
    )
    return (newbest, total, accum)


def attend_keys(carry, queries, keys_rows, values_rows):
    count = keys_rows.shape[0]
    if count > 1024 and count % 1024 == 0:
        blocks = count // 1024
        keys_split = keys_rows.reshape(blocks, 1024, keys_rows.shape[1])
        values_split = values_rows.reshape(blocks, 1024, values_rows.shape[1])

        def advance(state, pair):
            return (attend_block(state, queries, pair[0], pair[1]), None)

        carry, unused = lax.scan(advance, carry, (keys_split, values_split))
        return carry
    return attend_block(carry, queries, keys_rows, values_rows)


def start_state(queries):
    rows = queries.shape[0]
    heads_here = queries.shape[1]
    best = jnp.full((heads_here, rows), -1e30, jnp.float32)
    total = jnp.zeros((heads_here, rows), jnp.float32)
    accum = jnp.zeros(queries.shape, jnp.float32)
    return (best, total, accum)


def finish_state(state):
    best, total, accum = state
    result = accum / jnp.transpose(total)[..., None]
    return result.reshape(result.shape[0], result.shape[1] * result.shape[2]).astype(jnp.bfloat16)


def shards(
    tokens, modulation, w_qkv, w_out, w_cross, q_gain, k_gain, cross_gain, scene_keys, scene_values
):
    width = tokens.shape[1]
    local_width = w_qkv.shape[2]
    heads_here = local_width // HD
    rows_raw = lax.all_gather(tokens, "head", axis=0, tiled=True)
    rows_count = rows_raw.shape[0]
    xfloat = rows_raw.astype(jnp.float32)
    mean = jnp.mean(xfloat, axis=-1, keepdims=True)
    var = jnp.mean((xfloat - mean) ** 2, axis=-1, keepdims=True)
    normed = (xfloat - mean) * lax.rsqrt(var + 1e-06)
    modulated = (normed * (1.0 + modulation[1]) + modulation[0]).astype(jnp.bfloat16)
    projected = jnp.dot(
        modulated, w_qkv.reshape(width, 3 * local_width), preferred_element_type=jnp.float32
    )
    projected = projected.reshape(rows_count, 3, heads_here, HD)
    queries = head_norm(projected[:, 0], q_gain).astype(jnp.bfloat16)
    keys_flat = (
        head_norm(projected[:, 1], k_gain).astype(jnp.bfloat16).reshape(rows_count, local_width)
    )
    values_flat = projected[:, 2].astype(jnp.bfloat16).reshape(rows_count, local_width)
    pieces = (
        lax.all_gather(keys_flat, "blk", axis=0, tiled=True),
        lax.all_gather(values_flat, "blk", axis=0, tiled=True),
    )
    state = attend_keys(start_state(queries), queries, pieces[0], pieces[1])
    context = finish_state(state)
    partial_sum = jnp.dot(context, w_out, preferred_element_type=jnp.float32)
    mine = lax.psum_scatter(partial_sum, "head", scatter_dimension=0, tiled=True)
    hidden = (tokens.astype(jnp.float32) + modulation[2] * mine).astype(jnp.bfloat16)
    hidden_all = lax.all_gather(hidden, "head", axis=0, tiled=True)
    cross_proj = jnp.dot(hidden_all, w_cross, preferred_element_type=jnp.float32).reshape(
        rows_count, heads_here, HD
    )
    cross_queries = head_norm(cross_proj, cross_gain).astype(jnp.bfloat16)
    pieces = (
        lax.all_gather(scene_keys, "blk", axis=0, tiled=True),
        lax.all_gather(scene_values, "blk", axis=0, tiled=True),
    )
    scene_state = attend_keys(start_state(cross_queries), cross_queries, pieces[0], pieces[1])
    cross_context = finish_state(scene_state)
    return (hidden, cross_context)


def solution(mesh):
    return jax.shard_map(
        shards,
        mesh=mesh,
        in_specs=(
            P(("clip", "blk", "head"), None),
            P("clip", None),
            P(None, None, "head"),
            P("head", None),
            P(None, "head"),
            P(),
            P(),
            P(),
            P(("clip", "blk"), "head"),
            P(("clip", "blk"), "head"),
        ),
        out_specs=(P(("clip", "blk", "head"), None), P(("clip", "blk"), "head")),
        check_vma=False,
    )
```

profile of v0, /device:TPU:0, one launch (start us, length us, event | category | flops | bytes accessed | tf_op | source)
XLA Modules:
  0.0 181.9 jit_solution(1748630479518706990)
XLA Ops:
  7.2 2.9 %all_gather.18 = bf16[288,1536]{1,0:T(8,128)(2,1)S(1)} all-gather(bf16[144,1536]{1,0:T(8,128)(2,1)} %param.10), channel_id=1, replica_groups=mesh['blk'=4,'head'=2,'clip'=4] {'head'}, dimensions={0}, use_global_device_ids=true | all-gather | bytes 1327104 | tf_op jit(solution)/shard_map/all_gather | solution.py:70
  10.8 10.3 %copy.45 = bf16[1536,3,768]{0,2,1:T(8,128)(2,1)} copy(bf16[1536,3,768]{2,0,1:T(8,128)(2,1)} %param.12) | data formatting | bytes 14155776 | tf_op args[2]
  21.1 5.0 %fusion.23 = f32[288,3,6,128]{3,0,2,1:T(8,128)S(1)} fusion(bf16[3,6,128,1536]{3,2,1,0:T(8,128)(2,1)} %bitcast.93, bf16[288,1536]{1,0:T(8,128)(2,1)S(1)} %all_gather.18, f32[1536]{0:T(1024)S(1)} %get-tuple-element.3, f32[1536]{0:T(1024)S(1)} %get-tuple-element.4, f32[288]{0:T(512)S(1)} %add_rsqrt_fusion.3, f32[288]{0:T(512)S(1)} %broadcast_multiply_fusion), kind=kOutput, calls=%fused_computation.31 | convolution fusion | flops 2041085952 | bytes 10631424 | tf_op jit(solution)/shard_map/dot_general | solution.py:77
  26.1 1.5 copy-done.2
  29.1 1.0 fusion.26
  30.2 1.2 slice.39
  31.7 0.8 copy.84
  32.6 1.6 multiply_reduce_fusion.4
  34.1 39.0 %all-gather.3.cloned.1.call-done = bf16[1152,768]{1,0:T(8,128)(2,1)} async-done(((bf16[288,768]{1,0:T(8,128)(2,1)}), bf16[1152,768]{1,0:T(8,128)(2,1)}) %all-gather.3.cloned.1.call-update) | async-done | bytes 1769488 | tf_op jit(solution)/shard_map/all_gather | solution.py:87
  73.2 3.9 %copy.48 = bf16[1152,768]{0,1:T(8,128)(2,1)} copy(bf16[1152,768]{1,0:T(8,128)(2,1)} %all-gather.3.cloned.1.call-done) | data formatting | bytes 3538944 | tf_op jit(solution)/shard_map/all_gather | solution.py:87
  77.0 3.1 %multiply_reduce_fusion = (f32[6,288]{1,0:T(8,128)S(1)}, f32[6,288,1152]{2,1,0:T(8,128)S(1)}) fusion(bf16[1152,6,128]{0,2,1:T(8,128)(2,1)} %bitcast.94, f32[288,3,6,128]{3,0,2,1:T(8,128)} %copy-done.2, f32[128]{0:T(128)S(1)} %copy-done.10, f32[288,6]{0,1:T(8,128)S(1)} %add_rsqrt_fusion.2), kind=kOutput, calls=%fused_computation.1 | convolution fusion | flops 514251072 | bytes 10631168 | tf_op jit(solution)/shard_map/rhd,nhd->hrn/dot_general | solution.py:21
  80.2 1.8 %fusion = f32[6,288]{1,0:T(8,128)S(1)} fusion(f32[6,288,1152]{2,1,0:T(8,128)S(1)} %get-tuple-element.12, f32[6,288]{1,0:T(8,128)S(1)} %get-tuple-element.10), kind=kLoop, calls=%fused_computation.2 | loop fusion | flops 5970240 | bytes 7976448 | tf_op jit(solution)/shard_map/reduce_sum | solution.py:27
  82.0 1.2 copy-done.1
  83.3 31.2 %all-gather.5.cloned.1.call-done = bf16[1152,768]{1,0:T(8,128)(2,1)} async-done(((bf16[288,768]{1,0:T(8,128)(2,1)}), bf16[1152,768]{1,0:T(8,128)(2,1)}) %all-gather.5.cloned.1.call-update) | async-done | bytes 1769488 | tf_op jit(solution)/shard_map/all_gather | solution.py:88
  114.4 3.9 %copy.51 = bf16[1152,768]{0,1:T(8,128)(2,1)} copy(bf16[1152,768]{1,0:T(8,128)(2,1)} %all-gather.5.cloned.1.call-done) | data formatting | bytes 3538944 | tf_op jit(solution)/shard_map/all_gather | solution.py:88
  118.3 5.4 %fusion.21 = bf16[6,36,8,128]{3,2,1,0:T(8,128)(2,1)S(1)} fusion(bf16[1152,6,128]{0,2,1:T(8,128)(2,1)} %bitcast.98, f32[6,288,1152]{2,1,0:T(8,128)} %copy-done.1, f32[6,288]{1,0:T(8,128)S(1)} %get-tuple-element.10, f32[288,6]{0,1:T(8,128)S(1)} %bitcast_add_fusion.1, f32[288,6]{0,1:T(8,128)S(1)} %get-tuple-element.9), kind=kOutput, calls=%fused_computation.29 | convolution fusion | flops 514252800 | bytes 10195200 | tf_op jit(solution)/shard_map/hrn,nhd->rhd/dot_general | solution.py:28
  123.7 2.1 %fusion.34 = f32[288,1536]{1,0:T(8,128)} fusion(bf16[768,1536]{1,0:T(8,128)(2,1)S(1)} %copy-done, bf16[6,36,8,128]{3,2,1,0:T(8,128)(2,1)S(1)} %fusion.21), kind=kOutput, calls=%fused_computation.50 | convolution fusion | flops 679477248 | bytes 4571136 | tf_op jit(solution)/shard_map/dot_general | solution.py:92
  125.8 0.9 copy-done.7
  126.7 15.4 %all_gather.22 = bf16[256,768]{1,0:T(8,128)(2,1)S(1)} all-gather(bf16[64,768]{1,0:T(8,128)(2,1)S(1)} %copy-done.7), channel_id=1, replica_groups=mesh['blk'=4,'head'=2,'clip'=4] {'blk'}, dimensions={0}, use_global_device_ids=true | all-gather | bytes 491520 | tf_op jit(solution)/shard_map/all_gather | solution.py:101
  142.1 0.9 copy.56
  143.0 14.9 %all_gather.23 = bf16[256,768]{1,0:T(8,128)(2,1)S(1)} all-gather(bf16[64,768]{1,0:T(8,128)(2,1)S(1)} %copy-done.8), channel_id=1, replica_groups=mesh['blk'=4,'head'=2,'clip'=4] {'blk'}, dimensions={0}, use_global_device_ids=true | all-gather | bytes 491520 | tf_op jit(solution)/shard_map/all_gather | solution.py:102
  157.9 0.9 copy.59
  158.9 1.4 add_convert_fusion
  161.1 2.6 %all_gather.21 = bf16[288,1536]{1,0:T(8,128)(2,1)S(1)} all-gather(bf16[144,1536]{1,0:T(8,128)(2,1)S(1)} %add_convert_fusion), channel_id=1, replica_groups=mesh['blk'=4,'head'=2,'clip'=4] {'head'}, dimensions={0}, use_global_device_ids=true | all-gather | bytes 1327104 | tf_op jit(solution)/shard_map/all_gather | solution.py:95
  163.7 1.8 fusion.44
  165.5 1.3 reshape.88
  166.8 1.0 multiply_reduce_fusion.2
  167.8 1.0 copy.54
  169.4 1.5 copy.55
  170.9 1.3 multiply_convert_fusion
  173.6 0.9 fusion.18
  174.5 0.8 copy.85
  (52 shorter events, 5.2 us)
Async XLA Ops:
  7.2 116.6 %copy-start = (bf16[768,1536]{1,0:T(8,128)(2,1)S(1)}, bf16[768,1536]{1,0:T(8,128)(2,1)}, u32[]{:S(2)}) copy-start(bf16[768,1536]{1,0:T(8,128)(2,1)} %param.13) | copy-start | bytes 7077892
  7.2 3.6 %copy-start.9 = (f32[3,1536]{1,0:T(4,128)S(1)}, f32[3,1536]{1,0:T(4,128)}, u32[]{:S(2)}) copy-start(f32[3,1536]{1,0:T(4,128)} %param.11) | copy-start | bytes 55300
  7.2 66.0 %all-gather.3.cloned.1.call-start = ((), (), s32[]{:S(2)}) async-start(), calls=%async_computation.1 | async-start | bytes 2211840 | tf_op jit(solution)/shard_map/all_gather | solution.py:87
  26.1 1.5 copy-start.2
  27.6 1.1 copy-start.12
  30.2 84.3 %all-gather.5.cloned.1.call-start = ((), (), s32[]{:S(2)}) async-start(), calls=%async_computation.2 | async-start | bytes 2211840 | tf_op jit(solution)/shard_map/all_gather | solution.py:88
  32.5 126.4 %reduce-scatter.2.cloned.1.call-start = ((), (), s32[]{:S(2)}) async-start(), calls=%async_computation.3 | async-start | bytes 2654208 | tf_op jit(solution)/shard_map/reduce_scatter | solution.py:93
  34.1 42.9 %copy-start.10 = (f32[128]{0:T(128)S(1)}, f32[128]{0:T(128)}, u32[]{:S(2)}) copy-start(f32[128]{0:T(128)} %param.15) | copy-start | bytes 1540
  80.2 3.1 %copy-start.1 = (f32[6,288,1152]{2,1,0:T(8,128)}, f32[6,288,1152]{2,1,0:T(8,128)S(1)}, u32[]{:S(2)}) copy-start(f32[6,288,1152]{2,1,0:T(8,128)S(1)} %get-tuple-element.12) | copy-start | bytes 23887876
  125.8 0.9 copy-start.7
  125.8 17.2 %copy-start.8 = (bf16[64,768]{1,0:T(8,128)(2,1)S(1)}, bf16[64,768]{1,0:T(8,128)(2,1)}, u32[]{:S(2)}) copy-start(bf16[64,768]{1,0:T(8,128)(2,1)} %param.19) | copy-start | bytes 294916
  125.8 33.1 %copy-start.3 = (bf16[144,1536]{1,0:T(8,128)(2,1)S(1)}, bf16[144,1536]{1,0:T(8,128)(2,1)}, u32[]{:S(2)}) copy-start(bf16[144,1536]{1,0:T(8,128)(2,1)} %param.10) | copy-start | bytes 1327108
  158.9 4.8 %copy-start.13 = (bf16[1536,768]{1,0:T(8,128)(2,1)S(1)}, bf16[1536,768]{1,0:T(8,128)(2,1)}, u32[]{:S(2)}) copy-start(bf16[1536,768]{1,0:T(8,128)(2,1)} %param.14) | copy-start | bytes 7077892
  160.3 0.8 copy-start.4
  165.4 5.5 %copy-start.11 = (f32[128]{0:T(128)S(1)}, f32[128]{0:T(128)}, u32[]{:S(2)}) copy-start(f32[128]{0:T(128)} %param.17) | copy-start | bytes 1540
  170.9 1.3 copy-start.5
  172.3 1.3 copy-start.6
Sparse Core Ops, SparseCore 0:
  30.3 42.8 all-gather.2
  75.3 39.0 all-gather.4
  126.0 8.1 reduce-scatter.1
where the time goes:
time: 183 us; the launch traced here: 182 us
  waiting for transfers between devices  70.3 us (38%)
  blocking collectives  35.8 us (20%)
  local copies, waits for them, and re-layouts  32.2 us (18%)
  matrix products  18.8 us (10%)
  between operations  14 us (8%)
  other arithmetic  10.7 us (6%)
    all_gather x1, waiting for transfers between devices, shards(): lax.all_gather(keys_flat, 'blk', axis=0, tiled=True)  39 us
    all_gather x1, waiting for transfers between devices, shards(): lax.all_gather(values_flat, 'blk', axis=0, tiled=True)  31.2 us
    unnamed x30, local copies, waits for them, and re-layouts  15.5 us
    all_gather x1, blocking collectives, shards(): lax.all_gather(scene_keys, 'blk', axis=0, tiled=True)  15.4 us
    all_gather x1, blocking collectives, shards(): lax.all_gather(scene_values, 'blk', axis=0, tiled=True)  14.9 us
    dot_general x2, matrix products, attend_block(): jnp.einsum('hrn,nhd->rhd', weights, values_three)  6.29 us
    dot_general x1, matrix products, shards(): jnp.dot(modulated, w_qkv.reshape(width, 3 * local_width), preferred_eleme...  4.98 us
    all_gather x1, local copies, waits for them, and re-layouts, shards(): lax.all_gather(values_flat, 'blk', axis=0, tiled=True)  3.88 us
  transfers between devices with their start and end apart: 3, of which 2 were waited for; matrix products, arithmetic and copies ran while one was open for 8% of the time, Pallas kernels for 0%

commit v1 on v0

--- a/solution.py
+++ b/solution.py
@@ -4,6 +4,19 @@
 from jax.sharding import PartitionSpec as P
 
 HD = 128
+
+
+def collect(shard, axis, dim):
+    length, index, rows = (lax.axis_size(axis), lax.axis_index(axis), shard.shape[dim])
+    ahead = [(i, (i + 1) % length) for i in range(length)]
+    out = jnp.zeros((*shard.shape[:dim], length * rows, *shard.shape[dim + 1 :]), shard.dtype)
+    current = shard
+    for step in range(length):
+        source = (index - step) % length
+        out = lax.dynamic_update_slice_in_dim(out, current, source * rows, axis=dim)
+        if step < length - 1:
+            current = lax.ppermute(current, axis, ahead)
+    return out
 
 
 def head_norm(values, gain):
@@ -83,10 +96,7 @@
         head_norm(projected[:, 1], k_gain).astype(jnp.bfloat16).reshape(rows_count, local_width)
     )
     values_flat = projected[:, 2].astype(jnp.bfloat16).reshape(rows_count, local_width)
-    pieces = (
-        lax.all_gather(keys_flat, "blk", axis=0, tiled=True),
-        lax.all_gather(values_flat, "blk", axis=0, tiled=True),
-    )
+    pieces = (lax.all_gather(keys_flat, "blk", axis=0, tiled=True), collect(values_flat, "blk", 0))
     state = attend_keys(start_state(queries), queries, pieces[0], pieces[1])
     context = finish_state(state)
     partial_sum = jnp.dot(context, w_out, preferred_element_type=jnp.float32)

time: 183 us -> 190 us (1.038)
  waiting for transfers between devices: 70.3 us -> 38.1 us
  local copies, waits for them, and re-layouts: 32.2 us -> 59.8 us
  starting transfers between devices: 0.12 us -> 13.5 us
  matrix products: 18.8 us -> 15.3 us
    all_gather x1, waiting for transfers between devices: 39 us -> 0.01 us  [shards(): lax.all_gather(keys_flat, 'blk', axis=0, tiled=True)]
    ppermute x0 -> x3, waiting for transfers between devices: none -> 38 us  [collect(): current = lax.ppermute(current, axis, ahead)]
    all_gather x1 -> x0, waiting for transfers between devices: 31.2 us -> none  [shards(): lax.all_gather(values_flat, 'blk', axis=0, tiled=True)]
    dynamic_update_slice x0 -> x4, local copies, waits for them, and re-layouts: none -> 28.1 us  [collect(): out = lax.dynamic_update_slice_in_dim(out, current, source * rows, axis=dim)]
    ppermute x0 -> x3, starting transfers between devices: none -> 13.4 us  [collect(): current = lax.ppermute(current, axis, ahead)]
    all_gather x1 -> x0, local copies, waits for them, and re-layouts: 3.88 us -> none  [shards(): lax.all_gather(values_flat, 'blk', axis=0, tiled=True)]
    dot_general x2, matrix products: 6.29 us -> 2.87 us  [attend_block(): jnp.einsum('hrn,nhd->rhd', weights, values_three)]
    ppermute x0 -> x3, local copies, waits for them, and re-layouts: none -> 2.93 us  [collect(): current = lax.ppermute(current, axis, ahead)]
  transfers between devices with their start and end apart: 3 -> 5, of which waited for: 2 -> 2; matrix products, arithmetic and copies ran while one was open for 8% -> 20% of each run, Pallas kernels for 0% -> 0%
where the time goes in v1:
time: 190 us; the launch traced here: 189 us
  local copies, waits for them, and re-layouts  59.8 us (31%)
  waiting for transfers between devices  38.1 us (20%)
  blocking collectives  36.8 us (19%)
  matrix products  15.3 us (8%)
  between operations  14.4 us (8%)
  starting transfers between devices  13.5 us (7%)
  other arithmetic  10.7 us (6%)
    ppermute x3, waiting for transfers between devices, collect(): current = lax.ppermute(current, axis, ahead)  38 us
    dynamic_update_slice x4, local copies, waits for them, and re-layouts, collect(): out = lax.dynamic_update_slice_in_dim(out, current, source * rows, axis=dim)  28.1 us
    all_gather x1, blocking collectives, shards(): lax.all_gather(scene_keys, 'blk', axis=0, tiled=True)  16.4 us
    all_gather x1, blocking collectives, shards(): lax.all_gather(scene_values, 'blk', axis=0, tiled=True)  15.1 us
    unnamed x34, local copies, waits for them, and re-layouts  14.3 us
    ppermute x3, starting transfers between devices, collect(): current = lax.ppermute(current, axis, ahead)  13.4 us
    dot_general x1, matrix products, shards(): jnp.dot(modulated, w_qkv.reshape(width, 3 * local_width), preferred_eleme...  4.98 us
    all_gather x1, local copies, waits for them, and re-layouts, shards(): lax.all_gather(keys_flat, 'blk', axis=0, tiled=True)  3.86 us
  transfers between devices with their start and end apart: 5, of which 2 were waited for; matrix products, arithmetic and copies ran while one was open for 20% of the time, Pallas kernels for 0%

profile of v1, /device:TPU:0, one launch (start us, length us, event | category | flops | bytes accessed | tf_op | source)
XLA Modules:
  0.0 188.6 jit_solution(14501841845538203790)
XLA Ops:
  7.2 2.9 %all_gather.15 = bf16[288,1536]{1,0:T(8,128)(2,1)S(1)} all-gather(bf16[144,1536]{1,0:T(8,128)(2,1)} %param.10), channel_id=1, replica_groups=mesh['blk'=4,'head'=2,'clip'=4] {'head'}, dimensions={0}, use_global_device_ids=true | all-gather | bytes 1327104 | tf_op jit(solution)/shard_map/all_gather | solution.py:83
  10.8 10.3 %copy.51 = bf16[1536,3,768]{0,2,1:T(8,128)(2,1)} copy(bf16[1536,3,768]{2,0,1:T(8,128)(2,1)} %param.12) | data formatting | bytes 14155776 | tf_op args[2]
  21.1 5.0 %fusion.23 = f32[288,3,6,128]{3,0,2,1:T(8,128)S(1)} fusion(bf16[3,6,128,1536]{3,2,1,0:T(8,128)(2,1)} %bitcast.93, bf16[288,1536]{1,0:T(8,128)(2,1)S(1)} %all_gather.15, f32[1536]{0:T(1024)S(1)} %get-tuple-element.3, f32[1536]{0:T(1024)S(1)} %get-tuple-element.4, f32[288]{0:T(512)S(1)} %add_rsqrt_fusion.3, f32[288]{0:T(512)S(1)} %broadcast_multiply_fusion), kind=kOutput, calls=%fused_computation.31 | convolution fusion | flops 2041085952 | bytes 10631424 | tf_op jit(solution)/shard_map/dot_general | solution.py:90
  26.1 1.5 copy-done.1
  29.1 1.0 fusion.26
  30.2 1.2 slice.39
  31.7 3.0 %collective-permute-start = (bf16[288,768]{1,0:T(8,128)(2,1)S(1)}, bf16[288,768]{1,0:T(8,128)(2,1)S(1)}, u32[]{:S(2)}, u32[]{:S(2)}) collective-permute-start(bf16[288,768]{1,0:T(8,128)(2,1)S(1)} %bitcast.99), channel_id=1, source_target_pairs={{0,8},{8,16},{16,24},{24,0},{1,9},{9,17},{17,25},{25,1},{2,10},{10... | collective-permute-start | bytes 1327112 | tf_op jit(solution)/shard_map/ppermute | solution.py:18
  34.7 15.2 %collective-permute-done = bf16[288,768]{1,0:T(8,128)(2,1)S(1)} collective-permute-done((bf16[288,768]{1,0:T(8,128)(2,1)S(1)}, bf16[288,768]{1,0:T(8,128)(2,1)S(1)}, u32[]{:S(2)}, u32[]{:S(2)}) %collective-permute-start) | collective-permute-done | bytes 442400 | tf_op jit(solution)/shard_map/ppermute | solution.py:18
  50.7 3.7 %collective-permute-start.1 = (bf16[288,768]{1,0:T(8,128)(2,1)S(1)}, bf16[288,768]{1,0:T(8,128)(2,1)}, u32[]{:S(2)}, u32[]{:S(2)}) collective-permute-start(bf16[288,768]{1,0:T(8,128)(2,1)S(1)} %collective-permute-done), channel_id=1, source_target_pairs={{0,8},{8,16},{16,24},{24,0},{1,9},{9,17},{17,25},{25,1},{2,10},{10... | collective-permute-start | bytes 1327112 | tf_op jit(solution)/shard_map/ppermute | solution.py:18
  54.4 22.8 %collective-permute-done.1 = bf16[288,768]{1,0:T(8,128)(2,1)} collective-permute-done((bf16[288,768]{1,0:T(8,128)(2,1)S(1)}, bf16[288,768]{1,0:T(8,128)(2,1)}, u32[]{:S(2)}, u32[]{:S(2)}) %collective-permute-start.1) | collective-permute-done | bytes 442400 | tf_op jit(solution)/shard_map/ppermute | solution.py:18
  77.2 6.7 %collective-permute-start.2 = (bf16[288,768]{1,0:T(8,128)(2,1)}, bf16[288,768]{1,0:T(8,128)(2,1)}, u32[]{:S(2)}, u32[]{:S(2)}) collective-permute-start(bf16[288,768]{1,0:T(8,128)(2,1)} %collective-permute-done.1), channel_id=1, source_target_pairs={{0,8},{8,16},{16,24},{24,0},{1,9},{9,17},{17,25},{25,1},{2,10},{10... | collective-permute-start | bytes 1327112 | tf_op jit(solution)/shard_map/ppermute | solution.py:18
  84.4 1.3 broadcast_in_dim.2
  85.7 6.7 %dynamic_update_slice.12 = bf16[1152,768]{0,1:T(8,128)(2,1)} dynamic-update-slice(bf16[1152,768]{0,1:T(8,128)(2,1)} %broadcast_in_dim.2, bf16[288,768]{0,1:T(8,128)(2,1)S(1)} %copy.57, s32[]{:T(128)S(6)} %select_n.32, s32[]{:T(128)} %constant.63.clone.1) | dynamic-update-slice | bytes 884740 | tf_op jit(solution)/shard_map/dynamic_update_slice | solution.py:16
  92.4 1.6 multiply_reduce_fusion.4
  94.3 6.7 %dynamic_update_slice.13 = bf16[1152,768]{0,1:T(8,128)(2,1)} dynamic-update-slice(bf16[1152,768]{0,1:T(8,128)(2,1)} %dynamic_update_slice.12, bf16[288,768]{0,1:T(8,128)(2,1)S(1)} %copy.58, s32[]{:T(128)S(6)} %select_n.34, s32[]{:T(128)} %constant.63.clone.1) | dynamic-update-slice | bytes 884740 | tf_op jit(solution)/shard_map/dynamic_update_slice | solution.py:16
  101.0 1.3 copy.59
  102.3 7.3 %dynamic_update_slice.14 = bf16[1152,768]{0,1:T(8,128)(2,1)} dynamic-update-slice(bf16[1152,768]{0,1:T(8,128)(2,1)} %dynamic_update_slice.13, bf16[288,768]{0,1:T(8,128)(2,1)S(1)} %copy.59, s32[]{:T(128)S(6)} %select_n.36, s32[]{:T(128)} %constant.63.clone.1) | dynamic-update-slice | bytes 884740 | tf_op jit(solution)/shard_map/dynamic_update_slice | solution.py:16
  109.6 1.3 copy.60
  111.0 7.4 %dynamic_update_slice.15 = bf16[1152,768]{0,1:T(8,128)(2,1)} dynamic-update-slice(bf16[1152,768]{0,1:T(8,128)(2,1)} %dynamic_update_slice.14, bf16[288,768]{0,1:T(8,128)(2,1)S(1)} %copy.60, s32[]{:T(128)S(6)} %select_n.38, s32[]{:T(128)} %constant.63.clone.1) | dynamic-update-slice | bytes 884740 | tf_op jit(solution)/shard_map/dynamic_update_slice | solution.py:16
  118.3 3.9 %copy.54 = bf16[1152,768]{0,1:T(8,128)(2,1)} copy(bf16[1152,768]{1,0:T(8,128)(2,1)} %all-gather.2.cloned.1.call-done) | data formatting | bytes 3538944 | tf_op jit(solution)/shard_map/all_gather | solution.py:99
  122.2 3.1 %multiply_reduce_fusion = (f32[6,288]{1,0:T(8,128)S(1)}, f32[6,288,1152]{2,1,0:T(8,128)S(1)}) fusion(bf16[1152,6,128]{0,2,1:T(8,128)(2,1)} %bitcast.94, f32[288,3,6,128]{3,0,2,1:T(8,128)} %copy-done.1, f32[128]{0:T(128)S(1)} %copy-done.12, f32[288,6]{0,1:T(8,128)S(1)} %add_rsqrt_fusion.2), kind=kOutput, calls=%fused_computation.1 | convolution fusion | flops 514251072 | bytes 10631168 | tf_op jit(solution)/shard_map/rhd,nhd->hrn/dot_general | solution.py:34
  125.4 1.8 fusion
  127.2 2.0 %fusion.21 = bf16[6,36,8,128]{3,2,1,0:T(8,128)(2,1)S(1)} fusion(bf16[1152,6,128]{0,2,1:T(8,128)(2,1)S(1)} %bitcast.98, f32[6,288,1152]{2,1,0:T(8,128)S(1)} %get-tuple-element.12, f32[6,288]{1,0:T(8,128)S(1)} %get-tuple-element.10, f32[288,6]{0,1:T(8,128)S(1)} %bitcast_add_fusion.1, f32[288,6]{0,1:T(8,128)S(1)} %get-tuple-element.9), kind=kOutput, calls=%fused_computation.29 | convolution fusion | flops 514252800 | bytes 10195200 | tf_op jit(solution)/shard_map/hrn,nhd->rhd/dot_general | solution.py:41
  129.2 2.1 %fusion.34 = f32[288,1536]{1,0:T(8,128)} fusion(bf16[768,1536]{1,0:T(8,128)(2,1)S(1)} %copy-done, bf16[6,36,8,128]{3,2,1,0:T(8,128)(2,1)S(1)} %fusion.21), kind=kOutput, calls=%fused_computation.50 | convolution fusion | flops 679477248 | bytes 4571136 | tf_op jit(solution)/shard_map/dot_general | solution.py:102
  132.1 16.4 %all_gather.18 = bf16[256,768]{1,0:T(8,128)(2,1)S(1)} all-gather(bf16[64,768]{1,0:T(8,128)(2,1)S(1)} %copy-done.9), channel_id=1, replica_groups=mesh['blk'=4,'head'=2,'clip'=4] {'blk'}, dimensions={0}, use_global_device_ids=true | all-gather | bytes 491520 | tf_op jit(solution)/shard_map/all_gather | solution.py:111
  149.5 15.1 %all_gather.19 = bf16[256,768]{1,0:T(8,128)(2,1)S(1)} all-gather(bf16[64,768]{1,0:T(8,128)(2,1)S(1)} %copy-done.10), channel_id=1, replica_groups=mesh['blk'=4,'head'=2,'clip'=4] {'blk'}, dimensions={0}, use_global_device_ids=true | all-gather | bytes 491520 | tf_op jit(solution)/shard_map/all_gather | solution.py:112
  165.4 1.4 add_convert_fusion
  167.6 2.4 %all_gather.17 = bf16[288,1536]{1,0:T(8,128)(2,1)S(1)} all-gather(bf16[144,1536]{1,0:T(8,128)(2,1)S(1)} %add_convert_fusion), channel_id=1, replica_groups=mesh['blk'=4,'head'=2,'clip'=4] {'head'}, dimensions={0}, use_global_device_ids=true | all-gather | bytes 1327104 | tf_op jit(solution)/shard_map/all_gather | solution.py:105
  170.1 1.8 fusion.44
  171.8 1.3 reshape.88
  175.8 1.5 copy.64
  177.3 1.3 multiply_convert_fusion
  (67 shorter events, 13.1 us)
Async XLA Ops:
  7.2 122.0 %copy-start = (bf16[768,1536]{1,0:T(8,128)(2,1)S(1)}, bf16[768,1536]{1,0:T(8,128)(2,1)}, u32[]{:S(2)}) copy-start(bf16[768,1536]{1,0:T(8,128)(2,1)} %param.13) | copy-start | bytes 7077892
  7.2 3.6 %copy-start.11 = (f32[3,1536]{1,0:T(4,128)S(1)}, f32[3,1536]{1,0:T(4,128)}, u32[]{:S(2)}) copy-start(f32[3,1536]{1,0:T(4,128)} %param.11) | copy-start | bytes 55300
  7.2 111.2 %all-gather.2.cloned.1.call-start = ((), (), s32[]{:S(2)}) async-start(), calls=%async_computation.1 | async-start | bytes 2211840 | tf_op jit(solution)/shard_map/all_gather | solution.py:99
  26.1 1.5 copy-start.1
  27.6 1.1 copy-start.14
  30.2 135.3 %reduce-scatter.2.cloned.1.call-start = ((), (), s32[]{:S(2)}) async-start(), calls=%async_computation.2 | async-start | bytes 2654208 | tf_op jit(solution)/shard_map/reduce_scatter | solution.py:103
  31.7 18.2 %collective-permute-start = (bf16[288,768]{1,0:T(8,128)(2,1)S(1)}, bf16[288,768]{1,0:T(8,128)(2,1)S(1)}, u32[]{:S(2)}, u32[]{:S(2)}) collective-permute-start(bf16[288,768]{1,0:T(8,128)(2,1)S(1)} %bitcast.99), channel_id=1, source_target_pairs={{0,8},{8,16},{16,24},{24,0},{1,9},{9,17},{17,25},{25,1},{2,10},{10... | collective-permute-start | bytes 1327112 | tf_op jit(solution)/shard_map/ppermute | solution.py:18
  49.9 0.8 copy-start.6
  50.7 26.6 %collective-permute-start.1 = (bf16[288,768]{1,0:T(8,128)(2,1)S(1)}, bf16[288,768]{1,0:T(8,128)(2,1)}, u32[]{:S(2)}, u32[]{:S(2)}) collective-permute-start(bf16[288,768]{1,0:T(8,128)(2,1)S(1)} %collective-permute-done), channel_id=1, source_target_pairs={{0,8},{8,16},{16,24},{24,0},{1,9},{9,17},{17,25},{25,1},{2,10},{10... | collective-permute-start | bytes 1327112 | tf_op jit(solution)/shard_map/ppermute | solution.py:18
  77.2 32.4 %collective-permute-start.2 = (bf16[288,768]{1,0:T(8,128)(2,1)}, bf16[288,768]{1,0:T(8,128)(2,1)}, u32[]{:S(2)}, u32[]{:S(2)}) collective-permute-start(bf16[288,768]{1,0:T(8,128)(2,1)} %collective-permute-done.1), channel_id=1, source_target_pairs={{0,8},{8,16},{16,24},{24,0},{1,9},{9,17},{17,25},{25,1},{2,10},{10... | collective-permute-start | bytes 1327112 | tf_op jit(solution)/shard_map/ppermute | solution.py:18
  84.4 9.6 %copy-start.7 = (bf16[288,768]{1,0:T(8,128)(2,1)S(1)}, bf16[288,768]{1,0:T(8,128)(2,1)}, u32[]{:S(2)}) copy-start(bf16[288,768]{1,0:T(8,128)(2,1)} %copy-done.6) | copy-start | bytes 1327108
  118.3 3.9 %copy-start.12 = (f32[128]{0:T(128)S(1)}, f32[128]{0:T(128)}, u32[]{:S(2)}) copy-start(f32[128]{0:T(128)} %param.15) | copy-start | bytes 1540
  125.3 1.9 copy-start.4
  131.3 0.9 copy-start.9
  131.3 18.2 %copy-start.10 = (bf16[64,768]{1,0:T(8,128)(2,1)S(1)}, bf16[64,768]{1,0:T(8,128)(2,1)}, u32[]{:S(2)}) copy-start(bf16[64,768]{1,0:T(8,128)(2,1)} %param.19) | copy-start | bytes 294916
  131.3 34.2 %copy-start.2 = (bf16[144,1536]{1,0:T(8,128)(2,1)S(1)}, bf16[144,1536]{1,0:T(8,128)(2,1)}, u32[]{:S(2)}) copy-start(bf16[144,1536]{1,0:T(8,128)(2,1)} %param.10) | copy-start | bytes 1327108
  165.4 4.6 %copy-start.15 = (bf16[1536,768]{1,0:T(8,128)(2,1)S(1)}, bf16[1536,768]{1,0:T(8,128)(2,1)}, u32[]{:S(2)}) copy-start(bf16[1536,768]{1,0:T(8,128)(2,1)} %param.14) | copy-start | bytes 7077892
  166.9 0.8 copy-start.3
  171.8 5.5 %copy-start.13 = (f32[128]{0:T(128)S(1)}, f32[128]{0:T(128)}, u32[]{:S(2)}) copy-start(f32[128]{0:T(128)} %param.17) | copy-start | bytes 1540
  177.3 1.3 copy-start.5
  178.7 1.3 copy-start.8
Sparse Core Ops, SparseCore 0:
  30.3 55.3 all-gather.1
  131.4 10.5 reduce-scatter.1
